TPU v7x, 32 devices: a whole 2x2x4 slice. The times are simulated.
32 devices in a mesh: box: 8 (over z, y), nbr: 4 (over x, core).
Axes of the slice: x: 2, y: 2, z: 4, core: 2. Of those that a mesh axis runs over, the one named last changes fastest.
Arguments:
- self_block: float32 [64, 256, 256], P('box', 'nbr'), as said below
- ordering: int32 [64, 256], P('box'), may hold values from 0 to 255, each once within a row
- interp: float32 [64, 64, 192], P('box'), may hold values from -0.12 to 0.12
- near_band: float32 [64, 8, 2, 64, 256], P('box', 'nbr'), may hold values from -3 to 3
- pair_mask: int32 [64, 8], P('box', 'nbr'), may hold values 0 or 1
Outputs:
- skeleton_self: float32 [64, 64, 64], P('box')
- red_inverse: float32 [64, 192, 192], P('box', 'nbr')
- couplings: float32 [64, 8, 64, 128], P('box', 'nbr')
Inputs may be any that keep to these rules, and one draw needn't show every extreme that they name: Each row of ordering is a permutation of the 256 unknowns of its box. Each self_block[b] has a positive diagonal.
All inputs are finite; a program needn't handle non-finite values. No bound on the sum of `pair_mask` on one device may be relied on, other than what follows from the above.
Results may differ from a plain program's by a relative error of at most 0.0003.
Values sent between devices are 32-bit elements; how exact they have to be, the bound alone decides.
A program may use at most 128 MiB of HBM per device.

v0:
```python
import jax
import jax.numpy as jnp
from jax import lax
from jax.sharding import PartitionSpec as P

SKEL = 64
RED = 192
REACH = 4
NS_ITERS = 3


def extended_2(block, sides, width):
    for axis, dim in sides:
        count = lax.axis_size(axis)
        forward = [(i, i + 1) for i in range(count - 1)]
        forward.append((count - 1, 0))
        backward = [(target, source) for source, target in forward]
        low = lax.ppermute(
            lax.slice_in_dim(block, block.shape[dim] - width, None, axis=dim), axis, forward
        )
        high = lax.ppermute(lax.slice_in_dim(block, 0, width, axis=dim), axis, backward)
        block = jnp.concatenate([low, block, high], axis=dim)
    return block


def passed_along(block, axis, distance):
    devices = range(lax.axis_size(axis))
    route = [((i - distance) % len(devices), i) for i in devices]
    return lax.ppermute(block, axis, route)


def product(pattern, left_term, right_term):
    return jnp.einsum(pattern, left_term, right_term, precision=lax.Precision.HIGHEST)


def selector(ordering):
    columns = jnp.arange(ordering.shape[1], dtype=jnp.int32)
    return (ordering[:, :, None] == columns[None, None, :]).astype(jnp.float32)


def permuted(matrix, chooser):
    row_sorted = product("bik,bkj->bij", chooser, matrix)
    return product("bik,bjk->bij", row_sorted, chooser)


def factors(matrix, chooser, interp):
    full_block = permuted(matrix, chooser)
    skel_skel = full_block[:, :SKEL, :SKEL]
    skel_red = full_block[:, :SKEL, SKEL:]
    red_skel = full_block[:, SKEL:, :SKEL]
    red_red = full_block[:, SKEL:, SKEL:]
    skel_interp = product("bij,bjk->bik", skel_skel, interp)
    x_skel_red = skel_red - skel_interp
    x_red_skel = red_skel - product("bji,bjk->bik", interp, skel_skel)
    x_red_red = (
        red_red
        - product("bji,bjk->bik", interp, skel_red)
        - product("bij,bjk->bik", red_skel, interp)
    )
    x_red_red = x_red_red + product("bji,bjk->bik", interp, skel_interp)
    identity = jnp.eye(RED, dtype=jnp.float32)
    diag_vals = jnp.diagonal(red_red, axis1=1, axis2=2)
    approx = identity[None] / diag_vals[:, None, :]
    for sweep_index in range(NS_ITERS):
        approx = 2.0 * approx - product(
            "bij,bjk->bik", approx, product("bij,bjk->bik", x_red_red, approx)
        )
    left_factor = product("bij,bjk->bik", x_skel_red, approx)
    right_factor = product("bij,bjk->bik", approx, x_red_skel)
    own_block = skel_skel - product("bij,bjk->bik", left_factor, x_red_skel)
    return (approx, left_factor, right_factor, own_block)


def slot_terms(near_piece, chooser, interp, approx, left_factor, right_factor):
    both_parts = product("bpik,bjk->bpij", near_piece, chooser)
    row_part = both_parts[:, 0]
    col_part = both_parts[:, 1]
    near_red = row_part[:, :, SKEL:] - product("bij,bjk->bik", row_part[:, :, :SKEL], interp)
    red_near_t = col_part[:, :, SKEL:] - product("bij,bjk->bik", col_part[:, :, :SKEL], interp)
    new_forward = jnp.swapaxes(col_part[:, :, :SKEL], 1, 2) - product(
        "bij,bkj->bik", left_factor, red_near_t
    )
    new_backward = jnp.swapaxes(row_part[:, :, :SKEL], 1, 2) - product(
        "bji,bkj->bik", right_factor, near_red
    )
    coupled = jnp.concatenate([new_forward, new_backward], axis=2)
    update = product("bij,bkj->bik", product("bij,bjk->bik", near_red, approx), red_near_t)
    return (coupled, update)


def body(self_block, ordering, interp, near_band, pair_mask):
    box_count = ordering.shape[0]
    nbr_count = lax.axis_size("nbr")
    nbr_place = lax.axis_index("nbr")
    chooser = selector(ordering)
    share_boxes = box_count // nbr_count
    own_rows = lax.all_to_all(self_block, "nbr", split_axis=0, concat_axis=1, tiled=True)
    my_chooser = lax.dynamic_slice_in_dim(chooser, nbr_place * share_boxes, share_boxes, 0)
    my_interp = lax.dynamic_slice_in_dim(interp, nbr_place * share_boxes, share_boxes, 0)
    part_inverse, part_left, part_right, part_own = factors(own_rows, my_chooser, my_interp)
    approx, left_factor, right_factor, own_block = (
        lax.all_gather(part_inverse, "nbr", axis=0, tiled=True),
        lax.all_gather(part_left, "nbr", axis=0, tiled=True),
        lax.all_gather(part_right, "nbr", axis=0, tiled=True),
        lax.all_gather(part_own, "nbr", axis=0, tiled=True),
    )
    masked = near_band * pair_mask.astype(jnp.float32)[:, :, None, None, None]
    local_slots = near_band.shape[1]
    windows = []
    widened = extended_2(masked, (("box", 0),), REACH)
    for slot_index in range(local_slots):
        windows.append((widened[:, slot_index], REACH))
    extended = jnp.zeros((box_count + 2 * REACH, SKEL, SKEL), jnp.float32)
    couples = []
    for slot_index in range(local_slots):
        window, margin = windows[slot_index]
        global_slot = nbr_place * local_slots + slot_index
        offset = jnp.where(global_slot < REACH, global_slot - REACH, global_slot - REACH + 1)
        near_piece = lax.dynamic_slice_in_dim(window, margin - offset, box_count, 0)
        coupled, update = slot_terms(near_piece, chooser, interp, approx, left_factor, right_factor)
        couples.append(coupled)
        extended = extended + lax.dynamic_update_slice_in_dim(
            jnp.zeros_like(extended), update, REACH - offset, 0
        )
    incoming_right = passed_along(extended[:REACH], "box", -1)
    incoming_left = passed_along(extended[REACH + box_count :], "box", 1)
    owned_sum = extended[REACH : REACH + box_count]
    owned_sum = owned_sum.at[box_count - REACH :].add(incoming_right)
    owned_sum = owned_sum.at[:REACH].add(incoming_left)
    update_total = lax.psum(owned_sum, "nbr")
    skeleton_self = own_block - update_total
    row_count = approx.shape[1] // nbr_count
    red_inverse = lax.dynamic_slice_in_dim(approx, nbr_place * row_count, row_count, 1)
    return (skeleton_self, red_inverse, jnp.stack(couples, 1))


def solution(mesh):
    placed = (
        P("box", "nbr", None),
        P("box", None),
        P("box", None, None),
        P("box", "nbr", None, None, None),
        P("box", "nbr"),
    )
    return jax.shard_map(
        body,
        mesh=mesh,
        in_specs=placed,
        out_specs=(P("box", None, None), P("box", "nbr", None), P("box", "nbr", None, None)),
        check_vma=False,
    )
```

profile of v0, /device:TPU:0, one launch (start us, length us, event | category | flops | bytes accessed | tf_op | source)
XLA Modules:
  0.0 154.4 jit_solution(4811347467437603980)
XLA Ops:
  7.2 4.4 %all-to-all-start = ((f32[8,64,256]{2,1,0:T(8,128)}), f32[8,64,256]{2,1,0:T(8,128)S(1)}, u32[]{:S(2)}, u32[]{:S(2)}) async-start(f32[8,64,256]{2,1,0:T(8,128)} %param.9), calls=%async_computation | async-start | bytes 1048576 | tf_op jit(solution)/shard_map/all_to_all | solution.py:97
  11.6 0.7 convert_element_type.12
  12.2 0.1 copy.79
  12.3 1.9 %broadcast_multiply_fusion = f32[8,2,2,64,256]{4,3,2,1,0:T(8,128)S(1)} fusion(f32[8,2,2,64,256]{4,3,2,1,0:T(8,128)} %param.12, f32[8,2]{1,0:T(8,128)S(1)} %copy.79), kind=kLoop, calls=%fused_computation.31 | loop fusion | flops 524288 | bytes 4194368 | tf_op jit(solution)/shard_map/mul | solution.py:107
  14.2 1.5 fusion.50
  15.8 2.3 %collective-permute-start = (f32[4,2,2,64,256]{4,3,2,1,0:T(8,128)}, f32[4,2,2,64,256]{4,3,2,1,0:T(8,128)}, u32[]{:S(2)}, u32[]{:S(2)}) collective-permute-start(f32[4,2,2,64,256]{4,3,2,1,0:T(8,128)} %get-tuple-element.44), channel_id=1, source_target_pairs={{0,4},{4,8},{8,12},{12,16},{16,20},{20,24},{24,28},{28,0},{1,5},{5... | collective-permute-start | bytes 3145736 | tf_op jit(solution)/shard_map/ppermute | solution.py:18
  18.1 3.0 %collective-permute-start.1 = (f32[4,2,2,64,256]{4,3,2,1,0:T(8,128)}, f32[4,2,2,64,256]{4,3,2,1,0:T(8,128)}, u32[]{:S(2)}, u32[]{:S(2)}) collective-permute-start(f32[4,2,2,64,256]{4,3,2,1,0:T(8,128)} %get-tuple-element.45), channel_id=1, source_target_pairs={{4,0},{8,4},{12,8},{16,12},{20,16},{24,20},{28,24},{0,28},{5,1},{9... | collective-permute-start | bytes 3145736 | tf_op jit(solution)/shard_map/ppermute | solution.py:21
  21.1 0.7 fusion.25
  21.8 1.1 iota_compare_fusion
  23.0 1.4 fusion.12
  24.3 1.3 fusion.10
  25.7 0.6 convolution_subtract_fusion.5
  26.3 0.9 fusion.36
  27.2 0.9 slice.151
  28.1 0.7 slice.152
  28.8 0.5 convolution_subtract_fusion.4
  29.3 10.5 %copy.75 = f32[2,192,192]{0,2,1:T(8,128)} copy(f32[2,192,192]{2,1,0:T(8,128)} %slice.151) | data formatting | bytes 589824 | tf_op jit(solution)/shard_map/slice | solution.py:51
  39.8 5.2 %gather_fusion = f32[192,2]{1,0:T(8,128)} fusion(f32[2,192,192]{0,2,1:T(8,128)} %copy.75, s32[192]{0:T(256)S(1)} %bitcast.80), kind=kCustom, calls=%fused_computation | custom fusion | bytes 4608 | tf_op jit(solution)/shard_map/jit(diagonal)/gather | solution.py:62
  45.0 1.0 copy.76
  46.0 1.5 convolution_add_fusion
  47.5 1.5 fusion.14
  49.0 0.6 convolution_subtract_fusion.8
  49.5 0.5 fusion.52
  50.1 0.5 convolution_subtract_fusion.7
  50.6 0.5 fusion.53
  51.2 0.5 convolution_subtract_fusion.6
  51.7 2.1 %fusion.28 = f32[2,64,192]{2,1,0:T(8,128)} fusion(f32[2,192,192]{2,1,0:T(8,128)S(1)} %convolution_subtract_fusion.6, f32[2,64,192]{2,1,0:T(8,128)} %fusion.36, f32[2,256,256]{2,1,0:T(8,128)S(1)} %fusion.10), kind=kOutput, calls=%fused_computation.61 | convolution fusion | flops 56647680 | bytes 720896 | tf_op jit(solution)/shard_map/bij,bjk->bik/dot_general | solution.py:33
  53.8 0.0 all-reduce.2.cloned.1.call-start
  53.9 1.8 %copy.96 = f32[2,192,64]{1,2,0:T(8,128)} copy(f32[2,192,64]{2,1,0:T(8,128)} %slice.152) | data formatting | bytes 196608
  55.6 1.2 convolution_subtract_fusion.13
  56.9 1.2 convolution_subtract_fusion.14
  58.0 7.4 %all_gather.12 = f32[8,64,64]{2,1,0:T(8,128)} all-gather(f32[2,64,64]{2,1,0:T(8,128)S(1)} %convolution_subtract_fusion.14), channel_id=1, replica_groups=mesh['box'=8,'nbr'=4] {'nbr'}, dimensions={0}, use_global_device_ids=true | all-gather | bytes 163840 | tf_op jit(solution)/shard_map/all_gather | solution.py:105
  65.4 10.1 %all_gather.14 = f32[8,64,192]{2,1,0:T(8,128)S(1)} all-gather(f32[2,64,192]{2,1,0:T(8,128)} %fusion.28), channel_id=1, replica_groups=mesh['box'=8,'nbr'=4] {'nbr'}, dimensions={0}, use_global_device_ids=true | all-gather | bytes 491520 | tf_op jit(solution)/shard_map/all_gather | solution.py:103
  75.5 0.5 fusion.56
  76.0 7.5 %all_gather.15 = f32[8,192,64]{1,2,0:T(8,128)S(1)} all-gather(f32[2,192,64]{1,2,0:T(8,128)S(1)} %fusion.56), channel_id=1, replica_groups=mesh['box'=8,'nbr'=4] {'nbr'}, dimensions={0}, use_global_device_ids=true | all-gather | bytes 491520 | tf_op jit(solution)/shard_map/all_gather | solution.py:104
  83.5 2.0 %pad_maximum_fusion = f32[16,2,2,64,256]{4,3,2,1,0:T(8,128)S(1)} fusion(f32[4,2,2,64,256]{4,3,2,1,0:T(8,128)} %collective-permute-done.1, f32[8,2,2,64,256]{4,3,2,1,0:T(8,128)S(1)} %broadcast_multiply_fusion, f32[4,2,2,64,256]{4,3,2,1,0:T(8,128)} %collective-permute-done), kind=kLoop, calls=%fused_computation.1 | loop fusion | flops 2097152 | bytes 8388608 | tf_op jit(solution)/shard_map/concatenate | solution.py:22
  85.5 0.4 fusion.49
  85.9 1.6 %fusion.2 = f32[8,2,64,256]{3,2,0,1:T(8,128)S(1)} fusion(s32[8,256]{1,0:T(8,128)S(1)} %copy-done.14, f32[16,1,2,64,256]{4,3,2,1,0:T(8,128)S(1)} %get-tuple-element.42, s32[]{:T(128)S(6)} %select_n.30), kind=kOutput, calls=%fused_computation.5 | convolution fusion | flops 805830656 | bytes 2105348 | tf_op jit(solution)/shard_map/bpik,bjk->bpij/dot_general | solution.py:33
  87.5 0.1 slice_bitcast_fusion
  87.6 0.6 convolution_subtract_fusion
  88.2 1.6 %fusion = f32[8,2,64,256]{3,2,1,0:T(8,128)S(1)} fusion(f32[16,1,2,64,256]{4,3,2,1,0:T(8,128)S(1)} %get-tuple-element.43, s32[]{:T(128)S(6)} %select_n.28, s32[8,256]{1,0:T(8,128)S(1)} %copy-done.14), kind=kOutput, calls=%fused_computation.3 | convolution fusion | flops 805830656 | bytes 2105348 | tf_op jit(solution)/shard_map/bpik,bjk->bpij/dot_general | solution.py:33
  89.8 0.1 slice_bitcast_fusion.2
  89.9 0.6 convolution_subtract_fusion.1
  90.5 0.6 convolution_subtract_fusion.2
  91.1 0.6 convolution_subtract_fusion.3
  91.7 0.7 convolution_subtract_fusion.10
  92.4 0.7 convolution_subtract_fusion.12
  93.0 0.7 convolution_subtract_fusion.9
  93.7 0.7 convolution_subtract_fusion.11
  94.4 1.1 maximum_bitcast_fusion
  95.5 2.8 %fusion.54 = f32[8,64,192]{2,1,0:T(8,128)S(1)} fusion(f32[8,64,192]{2,1,0:T(8,128)} %copy-done.4, f32[8,192,192]{2,1,0:T(8,128)} %all-gather.2.cloned.1.call-done), kind=kOutput, calls=%fused_computation.89 | convolution fusion | flops 226492416 | bytes 1966080 | tf_op jit(solution)/shard_map/bij,bjk->bik/dot_general | solution.py:33
  98.3 0.6 convolution_dynamic-update-slice_fusion
  99.0 1.1 fusion.55
  100.2 0.6 fusion.4
  100.8 0.8 copy-done.7
  101.7 2.3 %collective-permute-start.2 = (f32[4,64,64]{2,1,0:T(8,128)S(1)}, f32[4,64,64]{2,1,0:T(8,128)S(1)}, u32[]{:S(2)}, u32[]{:S(2)}) collective-permute-start(f32[4,64,64]{2,1,0:T(8,128)S(1)} %get-tuple-element.51), channel_id=1, source_target_pairs={{4,0},{8,4},{12,8},{16,12},{20,16},{24,20},{28,24},{0,28},{5,1},{9... | collective-permute-start | bytes 196616 | tf_op jit(solution)/shard_map/ppermute | solution.py:29
  103.9 1.1 pad_maximum_fusion.1
  105.0 2.4 %copy.87 = f32[8,2,64,128]{3,2,1,0:T(8,128)} copy(f32[8,2,64,128]{2,3,0,1:T(8,128)} %pad_maximum_fusion.1) | data formatting | bytes 1048576
  107.4 0.1 collective-permute-start.3
  107.5 8.1 %collective-permute-done.3 = f32[4,64,64]{2,1,0:T(8,128)S(1)} collective-permute-done((f32[4,64,64]{2,1,0:T(8,128)S(1)}, f32[4,64,64]{2,1,0:T(8,128)S(1)}, u32[]{:S(2)}, u32[]{:S(2)}) %collective-permute-start.3) | collective-permute-done | bytes 65568 | tf_op jit(solution)/shard_map/ppermute | solution.py:29
  115.7 0.7 copy-done.11
  116.4 0.8 constant_dynamic-slice_fusion
  117.2 28.7 %all-reduce.2.cloned.1.call-done = f32[8,64,64]{2,1,0:T(8,128)} async-done(((f32[8,64,64]{2,1,0:T(8,128)}), f32[8,64,64]{2,1,0:T(8,128)}) %all-reduce.2.cloned.1.call-update) | async-done | bytes 131088 | tf_op jit(solution)/shard_map/psum | solution.py:130
  145.9 1.7 %sub.80 = f32[8,64,64]{2,1,0:T(8,128)} subtract(f32[8,64,64]{2,1,0:T(8,128)S(1)} %copy-done.12, f32[8,64,64]{2,1,0:T(8,128)} %all-reduce.2.cloned.1.call-done) | non-fusion elementwise | flops 32768 | bytes 393216 | tf_op jit(solution)/shard_map/sub | solution.py:131
  (43 shorter events, 0.3 us)
Async XLA Ops:
  7.2 18.5 %copy-start = (f32[8,64,192]{2,1,0:T(8,128)S(1)}, f32[8,64,192]{2,1,0:T(8,128)}, u32[]{:S(2)}) copy-start(f32[8,64,192]{2,1,0:T(8,128)} %param.11) | copy-start | bytes 1179652
  7.2 15.8 %all-to-all-start = ((f32[8,64,256]{2,1,0:T(8,128)}), f32[8,64,256]{2,1,0:T(8,128)S(1)}, u32[]{:S(2)}, u32[]{:S(2)}) async-start(f32[8,64,256]{2,1,0:T(8,128)} %param.9), calls=%async_computation | async-start | bytes 1048576 | tf_op jit(solution)/shard_map/all_to_all | solution.py:97
  11.6 83.9 %all-gather.2.cloned.1.call-start = ((), (), s32[]{:S(2)}) async-start(), calls=%async_computation.1 | async-start | bytes 1966080 | tf_op jit(solution)/shard_map/all_gather | solution.py:102
  14.2 7.6 %copy-start.14 = (s32[8,256]{1,0:T(8,128)S(1)}, s32[8,256]{1,0:T(8,128)}, u32[]{:S(2)}) copy-start(s32[8,256]{1,0:T(8,128)} %param.10) | copy-start | bytes 24580
  15.8 67.7 %collective-permute-start = (f32[4,2,2,64,256]{4,3,2,1,0:T(8,128)}, f32[4,2,2,64,256]{4,3,2,1,0:T(8,128)}, u32[]{:S(2)}, u32[]{:S(2)}) collective-permute-start(f32[4,2,2,64,256]{4,3,2,1,0:T(8,128)} %get-tuple-element.44), channel_id=1, source_target_pairs={{0,4},{4,8},{8,12},{12,16},{16,20},{20,24},{24,28},{28,0},{1,5},{5... | collective-permute-start | bytes 3145736 | tf_op jit(solution)/shard_map/ppermute | solution.py:18
  18.1 65.4 %collective-permute-start.1 = (f32[4,2,2,64,256]{4,3,2,1,0:T(8,128)}, f32[4,2,2,64,256]{4,3,2,1,0:T(8,128)}, u32[]{:S(2)}, u32[]{:S(2)}) collective-permute-start(f32[4,2,2,64,256]{4,3,2,1,0:T(8,128)} %get-tuple-element.45), channel_id=1, source_target_pairs={{4,0},{8,4},{12,8},{16,12},{20,16},{24,20},{28,24},{0,28},{5,1},{9... | collective-permute-start | bytes 3145736 | tf_op jit(solution)/shard_map/ppermute | solution.py:21
  46.0 3.0 %copy-start.13 = (f32[192,192]{1,0:T(8,128)S(1)}, f32[192,192]{1,0:T(8,128)}, u32[]{:S(2)}) copy-start(f32[192,192]{1,0:T(8,128)} %fusion.25) | copy-start | bytes 442372
  51.7 2.1 %copy-start.2 = (f32[2,192,192]{2,1,0:T(8,128)}, f32[2,192,192]{2,1,0:T(8,128)S(1)}, u32[]{:S(2)}) copy-start(f32[2,192,192]{2,1,0:T(8,128)S(1)} %convolution_subtract_fusion.6) | copy-start | bytes 884740
  53.8 21.7 %copy-start.3 = (f32[2,192,192]{2,1,0:T(8,128)S(1)}, f32[2,192,192]{2,1,0:T(8,128)}, u32[]{:S(2)}) copy-start(f32[2,192,192]{2,1,0:T(8,128)} %copy-done.2) | copy-start | bytes 884740
  53.8 92.0 %all-reduce.2.cloned.1.call-start = ((), (), s32[]{:S(2)}) async-start(), calls=%async_computation.2 | async-start | bytes 524288 | tf_op jit(solution)/shard_map/psum | solution.py:130
  88.2 3.5 %copy-start.5 = (f32[8,64,192]{2,1,0:T(8,128)}, f32[8,64,192]{2,1,0:T(8,128)S(1)}, u32[]{:S(2)}) copy-start(f32[8,64,192]{2,1,0:T(8,128)S(1)} %convolution_subtract_fusion) | copy-start | bytes 1179652
  91.7 2.0 %copy-start.4 = (f32[8,64,192]{2,1,0:T(8,128)}, f32[8,64,192]{2,1,0:T(8,128)S(1)}, u32[]{:S(2)}) copy-start(f32[8,64,192]{2,1,0:T(8,128)S(1)} %convolution_subtract_fusion.3) | copy-start | bytes 1179652
  95.5 3.5 %copy-start.1 = (f32[8,192,192]{2,1,0:T(8,128)S(1)}, f32[8,192,192]{2,1,0:T(8,128)}, u32[]{:S(2)}) copy-start(f32[8,192,192]{2,1,0:T(8,128)} %all-gather.2.cloned.1.call-done) | copy-start | bytes 3538948
  98.3 1.8 %copy-start.6 = (f32[8,64,192]{2,1,0:T(8,128)S(1)}, f32[8,64,192]{2,1,0:T(8,128)}, u32[]{:S(2)}) copy-start(f32[8,64,192]{2,1,0:T(8,128)} %copy-done.5) | copy-start | bytes 1179652
  99.0 4.9 %copy-start.9 = (f32[8,1,64,128]{2,3,0,1:T(8,128)S(1)}, f32[8,1,64,128]{2,3,0,1:T(8,128)}, u32[]{:S(2)}) copy-start(f32[8,1,64,128]{2,3,0,1:T(8,128)} %get-tuple-element.52) | copy-start | bytes 786436
  99.0 4.9 %copy-start.10 = (f32[8,1,64,128]{2,3,0,1:T(8,128)S(1)}, f32[8,1,64,128]{2,3,0,1:T(8,128)}, u32[]{:S(2)}) copy-start(f32[8,1,64,128]{2,3,0,1:T(8,128)} %get-tuple-element.53) | copy-start | bytes 786436
  100.8 0.8 copy-start.7
  101.7 5.7 %copy-start.8 = (f32[16,64,64]{2,1,0:T(8,128)S(1)}, f32[16,64,64]{2,1,0:T(8,128)}, u32[]{:S(2)}) copy-start(f32[16,64,64]{2,1,0:T(8,128)} %copy-done.7) | copy-start | bytes 786436
  101.7 5.8 %collective-permute-start.2 = (f32[4,64,64]{2,1,0:T(8,128)S(1)}, f32[4,64,64]{2,1,0:T(8,128)S(1)}, u32[]{:S(2)}, u32[]{:S(2)}) collective-permute-start(f32[4,64,64]{2,1,0:T(8,128)S(1)} %get-tuple-element.51), channel_id=1, source_target_pairs={{4,0},{8,4},{12,8},{16,12},{20,16},{24,20},{28,24},{0,28},{5,1},{9... | collective-permute-start | bytes 196616 | tf_op jit(solution)/shard_map/ppermute | solution.py:29
  105.0 40.9 %copy-start.12 = (f32[8,64,64]{2,1,0:T(8,128)S(1)}, f32[8,64,64]{2,1,0:T(8,128)}, u32[]{:S(2)}) copy-start(f32[8,64,64]{2,1,0:T(8,128)} %all_gather.12) | copy-start | bytes 393220
  107.4 8.2 %collective-permute-start.3 = (f32[4,64,64]{2,1,0:T(8,128)S(1)}, f32[4,64,64]{2,1,0:T(8,128)S(1)}, u32[]{:S(2)}, u32[]{:S(2)}) collective-permute-start(f32[4,64,64]{2,1,0:T(8,128)S(1)} %get-tuple-element.50), channel_id=1, source_target_pairs={{28,0},{0,4},{4,8},{8,12},{12,16},{16,20},{20,24},{24,28},{29,1},{... | collective-permute-start | bytes 196616 | tf_op jit(solution)/shard_map/ppermute | solution.py:29
  115.7 0.7 copy-start.11
Sparse Core Ops, SparseCore 0:
  53.9 20.9 all-gather.1
  116.5 29.3 all-reduce.1
where the time goes:
time: 155 us; the launch traced here: 154 us
  waiting for transfers between devices  36.9 us (24%)
  matrix products  28.6 us (18%)
  local copies, waits for them, and re-layouts  27.1 us (17%)
  blocking collectives  24.9 us (16%)
  between operations  14.5 us (9%)
  starting transfers between devices  12.1 us (8%)
  other arithmetic  10.3 us (7%)
    psum x1, waiting for transfers between devices, body(): update_total = lax.psum(owned_sum, 'nbr')  28.7 us
    dot_general x30, matrix products, product(): jnp.einsum(pattern, left_term, right_term, precision=lax.Precision.HIGHEST)  28.6 us
    slice x2, local copies, waits for them, and re-layouts, factors(): red_red = full_block[:, SKEL:, SKEL:]  11.4 us
    all_gather x1, blocking collectives, body(): lax.all_gather(part_left, 'nbr', axis=0, tiled=True)  10.1 us
    ppermute x2, waiting for transfers between devices, passed_along(): return lax.ppermute(block, axis, route)  8.12 us
    all_gather x1, blocking collectives, body(): lax.all_gather(part_right, 'nbr', axis=0, tiled=True)  7.46 us
    all_gather x1, blocking collectives, body(): lax.all_gather(part_own, 'nbr', axis=0, tiled=True)  7.4 us
    unnamed x33, local copies, waits for them, and re-layouts  6.4 us
  transfers between devices with their start and end apart: 7, of which 2 were waited for; matrix products, arithmetic and copies ran while one was open for 37% of the time, Pallas kernels for 0%

commit v1 on v0

--- a/solution.py
+++ b/solution.py
@@ -127,7 +127,8 @@
     owned_sum = extended[REACH : REACH + box_count]
     owned_sum = owned_sum.at[box_count - REACH :].add(incoming_right)
     owned_sum = owned_sum.at[:REACH].add(incoming_left)
-    update_total = lax.psum(owned_sum, "nbr")
+    parts = lax.all_gather(owned_sum, "nbr", axis=0, tiled=False)
+    update_total = parts.sum(axis=0)
     skeleton_self = own_block - update_total
     row_count = approx.shape[1] // nbr_count
     red_inverse = lax.dynamic_slice_in_dim(approx, nbr_place * row_count, row_count, 1)

time: 155 us -> 131 us (0.85)
  waiting for transfers between devices: 36.9 us -> 7.05 us
  blocking collectives: 24.9 us -> 34.8 us
  other arithmetic: 10.3 us -> 8.48 us
    psum x1 -> x0, waiting for transfers between devices: 28.7 us -> none  [body(): update_total = lax.psum(owned_sum, 'nbr')]
    all_gather x0 -> x1, blocking collectives: none -> 9.85 us  [body(): parts = lax.all_gather(owned_sum, 'nbr', axis=0, tiled=False)]
    unnamed x33 -> x16, local copies, waits for them, and re-layouts: 6.4 us -> 4.83 us
  transfers between devices with their start and end apart: 7 -> 6, of which waited for: 2 -> 2; matrix products, arithmetic and copies ran while one was open for 37% -> 43% of each run, Pallas kernels for 0% -> 0%
where the time goes in v1:
time: 131 us
  blocking collectives  34.8 us (27%)
  matrix products  28.5 us (22%)
  local copies, waits for them, and re-layouts  25.6 us (20%)
  between operations  14.4 us (11%)
  starting transfers between devices  11.8 us (9%)
  other arithmetic  8.48 us (6%)
  waiting for transfers between devices  7.05 us (5%)
    dot_general x30, matrix products, product(): jnp.einsum(pattern, left_term, right_term, precision=lax.Precision.HIGHEST)  28.5 us
    slice x2, local copies, waits for them, and re-layouts, factors(): red_red = full_block[:, SKEL:, SKEL:]  11.4 us
    all_gather x1, blocking collectives, body(): lax.all_gather(part_left, 'nbr', axis=0, tiled=True)  10.5 us
    all_gather x1, blocking collectives, body(): parts = lax.all_gather(owned_sum, 'nbr', axis=0, tiled=False)  9.85 us
    all_gather x1, blocking collectives, body(): lax.all_gather(part_right, 'nbr', axis=0, tiled=True)  7.46 us
    ppermute x2, waiting for transfers between devices, passed_along(): return lax.ppermute(block, axis, route)  7.02 us
    all_gather x1, blocking collectives, body(): lax.all_gather(part_own, 'nbr', axis=0, tiled=True)  6.91 us
    gather x2, local copies, waits for them, and re-layouts, factors(): diag_vals = jnp.diagonal(red_red, axis1=1, axis2=2)  6.29 us
  transfers between devices with their start and end apart: 6, of which 2 were waited for; matrix products, arithmetic and copies ran while one was open for 43% of the time, Pallas kernels for 0%

profile of v1, /device:TPU:0, one launch (start us, length us, event | category | flops | bytes accessed | tf_op | source)
XLA Modules:
  0.0 130.6 jit_solution(10462875051046469908)
XLA Ops:
  7.2 4.4 %all-to-all-start = ((f32[8,64,256]{2,1,0:T(8,128)}), f32[8,64,256]{2,1,0:T(8,128)S(1)}, u32[]{:S(2)}, u32[]{:S(2)}) async-start(f32[8,64,256]{2,1,0:T(8,128)} %param.9), calls=%async_computation | async-start | bytes 1048576 | tf_op jit(solution)/shard_map/all_to_all | solution.py:97
  11.6 0.7 convert_element_type.12
  12.2 0.1 copy.79
  12.3 1.9 %broadcast_multiply_fusion = f32[8,2,2,64,256]{4,3,2,1,0:T(8,128)S(1)} fusion(f32[8,2,2,64,256]{4,3,2,1,0:T(8,128)} %param.12, f32[8,2]{1,0:T(8,128)S(1)} %copy.79), kind=kLoop, calls=%fused_computation.31 | loop fusion | flops 524288 | bytes 4194368 | tf_op jit(solution)/shard_map/mul | solution.py:107
  14.2 1.6 %fusion.51 = (f32[4,2,2,64,256]{4,3,2,1,0:T(8,128)}, f32[4,2,2,64,256]{4,3,2,1,0:T(8,128)}) fusion(f32[8,2,2,64,256]{4,3,2,1,0:T(8,128)S(1)} %broadcast_multiply_fusion), kind=kLoop, calls=%fused_computation.86 | loop fusion | bytes 4194304 | tf_op jit(solution)/shard_map/slice | solution.py:19
  15.8 2.3 %collective-permute-start = (f32[4,2,2,64,256]{4,3,2,1,0:T(8,128)}, f32[4,2,2,64,256]{4,3,2,1,0:T(8,128)}, u32[]{:S(2)}, u32[]{:S(2)}) collective-permute-start(f32[4,2,2,64,256]{4,3,2,1,0:T(8,128)} %get-tuple-element.44), channel_id=1, source_target_pairs={{0,4},{4,8},{8,12},{12,16},{16,20},{20,24},{24,28},{28,0},{1,5},{5... | collective-permute-start | bytes 3145736 | tf_op jit(solution)/shard_map/ppermute | solution.py:18
  18.1 3.0 %collective-permute-start.1 = (f32[4,2,2,64,256]{4,3,2,1,0:T(8,128)}, f32[4,2,2,64,256]{4,3,2,1,0:T(8,128)}, u32[]{:S(2)}, u32[]{:S(2)}) collective-permute-start(f32[4,2,2,64,256]{4,3,2,1,0:T(8,128)} %get-tuple-element.45), channel_id=1, source_target_pairs={{4,0},{8,4},{12,8},{16,12},{20,16},{24,20},{28,24},{0,28},{5,1},{9... | collective-permute-start | bytes 3145736 | tf_op jit(solution)/shard_map/ppermute | solution.py:21
  21.1 0.7 fusion.25
  21.8 1.1 iota_compare_fusion
  23.0 1.4 %fusion.12 = f32[2,256,256]{2,1,0:T(8,128)S(1)} fusion(f32[2,256,256]{2,1,0:T(8,128)S(1)} %bitcast.87, pred[8,256,256]{2,1,0:T(32,128)(4,1)} %iota_compare_fusion, s32[]{:T(128)S(6)} %select_n.26), kind=kOutput, calls=%fused_computation.42 | convolution fusion | flops 402653184 | bytes 1179652 | tf_op jit(solution)/shard_map/bik,bkj->bij/dot_general | solution.py:33
  24.4 1.3 %fusion.10 = f32[2,256,256]{2,1,0:T(8,128)S(1)} fusion(f32[2,256,256]{2,1,0:T(8,128)S(1)} %fusion.12, pred[8,256,256]{2,1,0:T(32,128)(4,1)} %iota_compare_fusion, s32[]{:T(128)S(6)} %select_n.26), kind=kOutput, calls=%fused_computation.40 | convolution fusion | flops 402653184 | bytes 1179652 | tf_op jit(solution)/shard_map/bik,bjk->bij/dot_general | solution.py:33
  25.7 0.6 convolution_subtract_fusion.5
  26.3 0.9 fusion.37
  27.2 0.9 slice.151
  28.1 0.7 slice.152
  28.8 0.5 convolution_subtract_fusion.4
  29.3 10.5 %copy.75 = f32[2,192,192]{0,2,1:T(8,128)} copy(f32[2,192,192]{2,1,0:T(8,128)} %slice.151) | data formatting | bytes 589824 | tf_op jit(solution)/shard_map/slice | solution.py:51
  39.8 5.3 %gather_fusion = f32[192,2]{1,0:T(8,128)} fusion(f32[2,192,192]{0,2,1:T(8,128)} %copy.75, s32[192]{0:T(256)S(1)} %bitcast.85), kind=kCustom, calls=%fused_computation | custom fusion | bytes 4608 | tf_op jit(solution)/shard_map/jit(diagonal)/gather | solution.py:62
  45.1 1.0 copy.76
  46.1 1.5 %convolution_add_fusion = f32[2,192,192]{2,1,0:T(8,128)S(1)} fusion(f32[2,192,192]{2,1,0:T(8,128)S(1)} %convolution_subtract_fusion.4, f32[2,64,192]{2,1,0:T(8,128)} %fusion.37, f32[8,64,192]{2,1,0:T(8,128)S(1)} %copy-done, s32[]{:T(128)S(6)} %select_n.26), kind=kOutput, calls=%fused_computation.12 | convolution fusion | flops 56696832 | bytes 917508 | tf_op jit(solution)/shard_map/bji,bjk->bik/dot_general | solution.py:33
  47.6 1.5 %fusion.14 = f32[2,192,192]{2,1,0:T(8,128)S(1)} fusion(f32[2,192,192]{2,1,0:T(8,128)S(1)} %convolution_add_fusion, f32[2,192]{1,0:T(2,128)S(1)} %copy.76, f32[192,192]{1,0:T(8,128)} %fusion.25), kind=kOutput, calls=%fused_computation.44 | convolution fusion | flops 169943040 | bytes 738816 | tf_op jit(solution)/shard_map/bij,bjk->bik/dot_general | solution.py:33
  49.1 0.6 convolution_subtract_fusion.8
  49.6 0.5 fusion.53
  50.2 0.5 convolution_subtract_fusion.7
  50.7 0.5 fusion.54
  51.2 0.5 convolution_subtract_fusion.6
  51.8 2.1 %fusion.29 = f32[2,64,192]{2,1,0:T(8,128)} fusion(f32[2,192,192]{2,1,0:T(8,128)S(1)} %convolution_subtract_fusion.6, f32[2,64,192]{2,1,0:T(8,128)} %fusion.37, f32[2,256,256]{2,1,0:T(8,128)S(1)} %fusion.10), kind=kOutput, calls=%fused_computation.62 | convolution fusion | flops 56647680 | bytes 720896 | tf_op jit(solution)/shard_map/bij,bjk->bik/dot_general | solution.py:33
  53.9 0.0 all-gather.2.cloned.1.call-update
  53.9 1.7 %copy.96 = f32[2,192,64]{1,2,0:T(8,128)} copy(f32[2,192,64]{2,1,0:T(8,128)} %slice.152) | data formatting | bytes 196608
  55.7 1.2 convolution_subtract_fusion.13
  56.9 1.2 convolution_subtract_fusion.14
  58.1 6.9 %all_gather.20 = f32[8,64,64]{2,1,0:T(8,128)S(1)} all-gather(f32[2,64,64]{2,1,0:T(8,128)S(1)} %convolution_subtract_fusion.14), channel_id=1, replica_groups=mesh['box'=8,'nbr'=4] {'nbr'}, dimensions={0}, use_global_device_ids=true | all-gather | bytes 163840 | tf_op jit(solution)/shard_map/all_gather | solution.py:105
  65.0 10.5 %all_gather.25 = f32[8,64,192]{2,1,0:T(8,128)S(1)} all-gather(f32[2,64,192]{2,1,0:T(8,128)} %fusion.29), channel_id=1, replica_groups=mesh['box'=8,'nbr'=4] {'nbr'}, dimensions={0}, use_global_device_ids=true | all-gather | bytes 491520 | tf_op jit(solution)/shard_map/all_gather | solution.py:103
  75.5 0.5 fusion.57
  76.1 7.5 %all_gather.26 = f32[8,192,64]{1,2,0:T(8,128)S(1)} all-gather(f32[2,192,64]{1,2,0:T(8,128)S(1)} %fusion.57), channel_id=1, replica_groups=mesh['box'=8,'nbr'=4] {'nbr'}, dimensions={0}, use_global_device_ids=true | all-gather | bytes 491520 | tf_op jit(solution)/shard_map/all_gather | solution.py:104
  83.5 2.0 %pad_maximum_fusion = f32[16,2,2,64,256]{4,3,2,1,0:T(8,128)S(1)} fusion(f32[4,2,2,64,256]{4,3,2,1,0:T(8,128)} %collective-permute-done.1, f32[8,2,2,64,256]{4,3,2,1,0:T(8,128)S(1)} %broadcast_multiply_fusion, f32[4,2,2,64,256]{4,3,2,1,0:T(8,128)} %collective-permute-done), kind=kLoop, calls=%fused_computation.1 | loop fusion | flops 2097152 | bytes 8388608 | tf_op jit(solution)/shard_map/concatenate | solution.py:22
  85.6 0.4 fusion.50
  86.0 1.6 %fusion.2 = f32[8,2,64,256]{3,2,0,1:T(8,128)S(1)} fusion(s32[8,256]{1,0:T(8,128)S(1)} %copy-done.5, f32[16,1,2,64,256]{4,3,2,1,0:T(8,128)S(1)} %get-tuple-element.42, s32[]{:T(128)S(6)} %select_n.30), kind=kOutput, calls=%fused_computation.5 | convolution fusion | flops 805830656 | bytes 2105348 | tf_op jit(solution)/shard_map/bpik,bjk->bpij/dot_general | solution.py:33
  87.6 0.1 slice_bitcast_fusion
  87.7 0.6 convolution_subtract_fusion
  88.3 0.6 convolution_subtract_fusion.1
  88.8 1.6 %fusion = f32[8,2,64,256]{3,2,1,0:T(8,128)S(1)} fusion(f32[16,1,2,64,256]{4,3,2,1,0:T(8,128)S(1)} %get-tuple-element.43, s32[]{:T(128)S(6)} %select_n.28, s32[8,256]{1,0:T(8,128)S(1)} %copy-done.5), kind=kOutput, calls=%fused_computation.3 | convolution fusion | flops 805830656 | bytes 2105348 | tf_op jit(solution)/shard_map/bpik,bjk->bpij/dot_general | solution.py:33
  90.4 0.1 slice_bitcast_fusion.2
  90.5 0.6 convolution_subtract_fusion.2
  91.1 0.6 convolution_subtract_fusion.3
  91.7 0.7 convolution_subtract_fusion.10
  92.4 0.7 convolution_subtract_fusion.12
  93.0 0.7 convolution_subtract_fusion.9
  93.7 0.7 convolution_subtract_fusion.11
  94.4 0.1 maximum_bitcast_fusion
  94.5 1.1 pad_maximum_fusion.1
  95.5 2.3 %copy.87 = f32[8,2,64,128]{3,2,1,0:T(8,128)} copy(f32[8,2,64,128]{2,3,0,1:T(8,128)} %pad_maximum_fusion.1) | data formatting | bytes 1048576
  97.9 2.6 %fusion.55 = f32[8,64,192]{2,1,0:T(8,128)S(1)} fusion(f32[8,64,192]{2,1,0:T(8,128)S(1)} %convolution_subtract_fusion.3, f32[8,192,192]{2,1,0:T(8,128)} %all-gather.2.cloned.1.call-done), kind=kOutput, calls=%fused_computation.90 | convolution fusion | flops 226492416 | bytes 1966080 | tf_op jit(solution)/shard_map/bij,bjk->bik/dot_general | solution.py:33
  100.6 0.6 convolution_dynamic-update-slice_fusion
  101.2 1.1 fusion.56
  102.4 0.6 fusion.4
  103.1 1.8 %collective-permute-start.2 = (f32[4,64,64]{2,1,0:T(8,128)S(1)}, f32[4,64,64]{2,1,0:T(8,128)S(1)}, u32[]{:S(2)}, u32[]{:S(2)}) collective-permute-start(f32[4,64,64]{2,1,0:T(8,128)S(1)} %get-tuple-element.51), channel_id=1, source_target_pairs={{4,0},{8,4},{12,8},{16,12},{20,16},{24,20},{28,24},{0,28},{5,1},{9... | collective-permute-start | bytes 196616 | tf_op jit(solution)/shard_map/ppermute | solution.py:29
  104.8 0.3 collective-permute-start.3
  105.2 0.8 constant_dynamic-slice_fusion
  105.9 2.9 %collective-permute-done.2 = f32[4,64,64]{2,1,0:T(8,128)S(1)} collective-permute-done((f32[4,64,64]{2,1,0:T(8,128)S(1)}, f32[4,64,64]{2,1,0:T(8,128)S(1)}, u32[]{:S(2)}, u32[]{:S(2)}) %collective-permute-start.2) | collective-permute-done | bytes 65568 | tf_op jit(solution)/shard_map/ppermute | solution.py:29
  108.9 4.1 %collective-permute-done.3 = f32[4,64,64]{2,1,0:T(8,128)S(1)} collective-permute-done((f32[4,64,64]{2,1,0:T(8,128)S(1)}, f32[4,64,64]{2,1,0:T(8,128)S(1)}, u32[]{:S(2)}, u32[]{:S(2)}) %collective-permute-start.3) | collective-permute-done | bytes 65568 | tf_op jit(solution)/shard_map/ppermute | solution.py:29
  113.0 9.9 %all_gather.24 = f32[4,8,64,64]{3,2,1,0:T(8,128)S(1)} all-gather(f32[1,8,64,64]{3,2,1,0:T(8,128)S(1)} %fusion.27), channel_id=1, replica_groups=mesh['box'=8,'nbr'=4] {'nbr'}, dimensions={0}, use_global_device_ids=true | all-gather | bytes 655360 | tf_op jit(solution)/shard_map/all_gather | solution.py:130
  122.9 0.1 reduce_sum.9
  123.0 0.7 sub.80
  (25 shorter events, 0.2 us)
Async XLA Ops:
  7.2 18.5 %copy-start = (f32[8,64,192]{2,1,0:T(8,128)S(1)}, f32[8,64,192]{2,1,0:T(8,128)}, u32[]{:S(2)}) copy-start(f32[8,64,192]{2,1,0:T(8,128)} %param.11) | copy-start | bytes 1179652
  7.2 15.8 %all-to-all-start = ((f32[8,64,256]{2,1,0:T(8,128)}), f32[8,64,256]{2,1,0:T(8,128)S(1)}, u32[]{:S(2)}, u32[]{:S(2)}) async-start(f32[8,64,256]{2,1,0:T(8,128)} %param.9), calls=%async_computation | async-start | bytes 1048576 | tf_op jit(solution)/shard_map/all_to_all | solution.py:97
  11.6 86.3 %all-gather.2.cloned.1.call-start = ((), (), s32[]{:S(2)}) async-start(), calls=%async_computation.1 | async-start | bytes 1966080 | tf_op jit(solution)/shard_map/all_gather | solution.py:102
  14.2 7.6 %copy-start.5 = (s32[8,256]{1,0:T(8,128)S(1)}, s32[8,256]{1,0:T(8,128)}, u32[]{:S(2)}) copy-start(s32[8,256]{1,0:T(8,128)} %param.10) | copy-start | bytes 24580
  15.8 67.7 %collective-permute-start = (f32[4,2,2,64,256]{4,3,2,1,0:T(8,128)}, f32[4,2,2,64,256]{4,3,2,1,0:T(8,128)}, u32[]{:S(2)}, u32[]{:S(2)}) collective-permute-start(f32[4,2,2,64,256]{4,3,2,1,0:T(8,128)} %get-tuple-element.44), channel_id=1, source_target_pairs={{0,4},{4,8},{8,12},{12,16},{16,20},{20,24},{24,28},{28,0},{1,5},{5... | collective-permute-start | bytes 3145736 | tf_op jit(solution)/shard_map/ppermute | solution.py:18
  18.1 65.5 %collective-permute-start.1 = (f32[4,2,2,64,256]{4,3,2,1,0:T(8,128)}, f32[4,2,2,64,256]{4,3,2,1,0:T(8,128)}, u32[]{:S(2)}, u32[]{:S(2)}) collective-permute-start(f32[4,2,2,64,256]{4,3,2,1,0:T(8,128)} %get-tuple-element.45), channel_id=1, source_target_pairs={{4,0},{8,4},{12,8},{16,12},{20,16},{24,20},{28,24},{0,28},{5,1},{9... | collective-permute-start | bytes 3145736 | tf_op jit(solution)/shard_map/ppermute | solution.py:21
  46.1 3.0 %copy-start.4 = (f32[192,192]{1,0:T(8,128)S(1)}, f32[192,192]{1,0:T(8,128)}, u32[]{:S(2)}) copy-start(f32[192,192]{1,0:T(8,128)} %fusion.25) | copy-start | bytes 442372
  51.8 2.1 %copy-start.2 = (f32[2,192,192]{2,1,0:T(8,128)}, f32[2,192,192]{2,1,0:T(8,128)S(1)}, u32[]{:S(2)}) copy-start(f32[2,192,192]{2,1,0:T(8,128)S(1)} %convolution_subtract_fusion.6) | copy-start | bytes 884740
  53.9 21.6 %copy-start.3 = (f32[2,192,192]{2,1,0:T(8,128)S(1)}, f32[2,192,192]{2,1,0:T(8,128)}, u32[]{:S(2)}) copy-start(f32[2,192,192]{2,1,0:T(8,128)} %copy-done.2) | copy-start | bytes 884740
  97.9 3.3 %copy-start.1 = (f32[8,192,192]{2,1,0:T(8,128)S(1)}, f32[8,192,192]{2,1,0:T(8,128)}, u32[]{:S(2)}) copy-start(f32[8,192,192]{2,1,0:T(8,128)} %all-gather.2.cloned.1.call-done) | copy-start | bytes 3538948
  103.1 5.8 %collective-permute-start.2 = (f32[4,64,64]{2,1,0:T(8,128)S(1)}, f32[4,64,64]{2,1,0:T(8,128)S(1)}, u32[]{:S(2)}, u32[]{:S(2)}) collective-permute-start(f32[4,64,64]{2,1,0:T(8,128)S(1)} %get-tuple-element.51), channel_id=1, source_target_pairs={{4,0},{8,4},{12,8},{16,12},{20,16},{24,20},{28,24},{0,28},{5,1},{9... | collective-permute-start | bytes 196616 | tf_op jit(solution)/shard_map/ppermute | solution.py:29
  104.8 8.2 %collective-permute-start.3 = (f32[4,64,64]{2,1,0:T(8,128)S(1)}, f32[4,64,64]{2,1,0:T(8,128)S(1)}, u32[]{:S(2)}, u32[]{:S(2)}) collective-permute-start(f32[4,64,64]{2,1,0:T(8,128)S(1)} %get-tuple-element.50), channel_id=1, source_target_pairs={{28,0},{0,4},{4,8},{8,12},{12,16},{16,20},{20,24},{24,28},{29,1},{... | collective-permute-start | bytes 196616 | tf_op jit(solution)/shard_map/ppermute | solution.py:29
Sparse Core Ops, SparseCore 0:
  54.0 21.4 all-gather.1
